TPU v7x, 256 devices: a whole 4x4x8 slice. The times are simulated.
256 devices in a mesh: tm: 16 (over y_hi, z), sub: 16 (over x, y_lo, core).
Axes of the slice: x: 4, y: 4 (y_hi: 2, y_lo: 2; y = y_hi * 2 + y_lo), z: 8, core: 2. Of those that a mesh axis runs over, the one named last changes fastest.
Arguments:
- frames: bfloat16 [16384, 1024], P(('tm', 'sub')), may hold values from -16 to 16
- modulation: float32 [8, 1024], replicated, may hold values from -4 to 4
- w_project: bfloat16 [3, 1024, 1024], P(None, None, 'sub'), may hold values from -1 to 1
- w_heads_out: bfloat16 [1024, 1024], P('sub'), may hold values from -0.25 to 0.25
- w_up: bfloat16 [1024, 4096], P(None, 'sub'), may hold values from -0.1875 to 0.1875
- w_down: bfloat16 [4096, 1024], P('sub'), may hold values from -0.125 to 0.125
- w_velocity: bfloat16 [1024, 100], replicated, may hold values from -0.1875 to 0.1875
- noisy_mel: float32 [16384, 100], P('tm'), may hold values from -6 to 6
- w_prelude: bfloat16 [7, 1536, 100], P(None, 'sub'), may hold values from -0.21875 to 0.21875
- w_upsample: bfloat16 [8, 1536, 768], P(None, 'sub'), may hold values from -0.109375 to 0.109375
- snake_alpha: float32 [2, 768], replicated, may hold values from 0.3 to 3
- w_dilated: bfloat16 [3, 768, 768], P(None, 'sub'), may hold values from -0.125 to 0.125
- w_plain: bfloat16 [3, 768, 768], P(None, 'sub'), may hold values from -0.125 to 0.125
Outputs:
- mel_next: float32 [16384, 100], P('tm')
- section_out: bfloat16 [65536, 768], P(('tm', 'sub'))
All inputs are finite; a program needn't handle non-finite values.
Results may differ from a plain program's by a relative error of at most 0.03.
Values may be sent and summed in bfloat16 or wider, within the bound.
No kernel may reach another device: no remote copies, remote signals or barrier semaphores. Data moves between devices by JAX's collectives and lax.ppermute only.
A program may use at most 64 MiB of HBM per device.

v0:
```python
import math
import jax
import jax.numpy as jnp
from jax import lax
from jax.sharding import PartitionSpec as P

HEAD_DIM = 64
BLK = 256
epsilon = 1e-06


def from_behind(block, axis, distance):
    devices = range(lax.axis_size(axis))
    route = [(i - distance, i) for i in devices if i - distance in devices]
    return lax.ppermute(block, axis, route)


def extended_2(cells, sides, width):
    for axis, dim in sides:
        count = lax.axis_size(axis)
        ends = count - 1
        head = lax.slice_in_dim(cells, 0, width, axis=dim)
        tail = lax.slice_in_dim(cells, cells.shape[dim] - width, cells.shape[dim], axis=dim)
        cells = jnp.concatenate(
            [
                lax.ppermute(tail, axis, [(i, (i + 1) % count) for i in range(ends)]),
                cells,
                lax.ppermute(head, axis, [((i + 1) % count, i) for i in range(ends)]),
            ],
            axis=dim,
        )
    return cells


def norm_rows(rows, offset_row, scale_row):
    rows = rows.astype(jnp.float32)
    center = jnp.mean(rows, axis=-1, keepdims=True)
    square = jnp.mean(rows * rows, axis=-1, keepdims=True)
    spread = square - center * center
    return (rows - center) * lax.rsqrt(spread + epsilon) * (1.0 + scale_row) + offset_row


def snake_act(values, alpha_row):
    return values + jnp.square(jnp.sin(alpha_row * values)) / alpha_row


def contract_first(left, right):
    return lax.dot_general(
        left, right, (((0,), (0,)), ((), ())), preferred_element_type=jnp.float32
    )


def phase_terms(prelude_cols, tap_weights, first_frame, span):
    current = lax.dynamic_slice_in_dim(prelude_cols, 1, span, 1)
    earlier = lax.dynamic_slice_in_dim(prelude_cols, first_frame, span, 1)
    later_frames = lax.dynamic_slice_in_dim(prelude_cols, 2, span, 1)

    def tap_product(source, offset):
        return contract_first(source, tap_weights[offset])

    phases = jnp.stack(
        [
            tap_product(current, 2) + tap_product(earlier, 6),
            tap_product(current, 3) + tap_product(earlier, 7),
            tap_product(current, 4) + tap_product(later_frames, 0),
            tap_product(current, 5) + tap_product(later_frames, 1),
        ],
        1,
    )
    return phases.reshape((4 * span, phases.shape[2]))


def block_attention(queries, keys_now, values_now, lookback, is_first):
    frame_count = queries.shape[0]
    head_count = queries.shape[1] // HEAD_DIM
    blocks = frame_count // BLK
    block_shape = (blocks, BLK, head_count, HEAD_DIM)
    edge_shape = (1, BLK, head_count, HEAD_DIM)
    key_blocks = keys_now.reshape(block_shape)
    value_blocks = values_now.reshape(block_shape)
    key_all = jnp.concatenate(
        [jnp.concatenate([lookback[0].reshape(edge_shape), key_blocks[:-1]], 0), key_blocks], 1
    )
    value_all = jnp.concatenate(
        [jnp.concatenate([lookback[1].reshape(edge_shape), value_blocks[:-1]], 0), value_blocks], 1
    )
    scores = jnp.einsum(
        "bqhd,bkhd->bhqk", queries.reshape(block_shape), key_all, preferred_element_type=jnp.float32
    ) / math.sqrt(HEAD_DIM)
    block_ids = lax.broadcasted_iota(jnp.int32, (blocks, 1, 1, 2 * BLK), 0)
    key_ids = lax.broadcasted_iota(jnp.int32, (blocks, 1, 1, 2 * BLK), 3)
    allowed = (block_ids > 0) | (key_ids >= BLK) | jnp.logical_not(is_first)
    scores = jnp.where(allowed, scores, -1e30)
    largest = jnp.max(scores, axis=-1, keepdims=True)
    raised = jnp.exp(scores - largest)
    weights = (raised / jnp.sum(raised, axis=-1, keepdims=True)).astype(jnp.bfloat16)
    attended = jnp.einsum("bhqk,bkhd->bqhd", weights, value_all, preferred_element_type=jnp.float32)
    return attended.reshape((frame_count, head_count * HEAD_DIM)).astype(jnp.bfloat16)


def dilated_conv(extended, row_count, w_dilated):
    empty_sum = jnp.zeros((row_count, w_dilated.shape[2]), jnp.float32)
    running = empty_sum
    weight_rows = lax.all_gather(w_dilated, "sub", axis=1, tiled=True)
    for offset in range(3):
        running = running + jnp.dot(
            extended[3 * offset : 3 * offset + row_count],
            weight_rows[offset],
            preferred_element_type=jnp.float32,
        )
    return running


def plain_conv(extended, row_count, w_plain):
    empty_sum = jnp.zeros((row_count, w_plain.shape[2]), jnp.float32)
    running = empty_sum
    weight_rows = lax.all_gather(w_plain, "sub", axis=1, tiled=True)
    for offset in range(3):
        running = running + jnp.dot(
            extended[offset : offset + row_count],
            weight_rows[offset],
            preferred_element_type=jnp.float32,
        )
    return running


def body(
    frames,
    modulation,
    w_project,
    w_heads_out,
    w_up,
    w_down,
    w_velocity,
    noisy_mel,
    w_prelude,
    w_upsample,
    snake_alpha,
    w_dilated,
    w_plain,
):
    own_rows = frames.shape[0]
    sub_index = lax.axis_index("sub")
    time_index = lax.axis_index("tm")
    gathered = lax.all_gather(frames, "sub", axis=0, tiled=True)
    frame_count = gathered.shape[0]
    first_norm = norm_rows(gathered, modulation[0], modulation[1]).astype(jnp.bfloat16)
    projected = jnp.einsum(
        "td,kde->kte", first_norm, w_project, preferred_element_type=jnp.float32
    ).astype(jnp.bfloat16)
    lookback = from_behind(
        (projected[1, frame_count - BLK :], projected[2, frame_count - BLK :]), "tm", 1
    )
    heads_out = block_attention(projected[0], projected[1], projected[2], lookback, time_index == 0)
    attn = lax.psum_scatter(
        jnp.dot(heads_out, w_heads_out, preferred_element_type=jnp.float32).astype(jnp.bfloat16),
        "sub",
        scatter_dimension=0,
        tiled=True,
    ).astype(jnp.float32)
    mixed_rows = (frames.astype(jnp.float32) + modulation[2] * attn).astype(jnp.bfloat16)
    own_norm = norm_rows(mixed_rows, modulation[3], modulation[4]).astype(jnp.bfloat16)
    second_norm = lax.all_gather(own_norm, "sub", axis=0, tiled=True)
    hidden = jax.nn.gelu(
        jnp.dot(second_norm, w_up, preferred_element_type=jnp.float32), approximate=True
    ).astype(jnp.bfloat16)
    feed = lax.psum_scatter(
        jnp.dot(hidden, w_down, preferred_element_type=jnp.float32).astype(jnp.bfloat16),
        "sub",
        scatter_dimension=0,
        tiled=True,
    ).astype(jnp.float32)
    final_rows = (mixed_rows.astype(jnp.float32) + modulation[5] * feed).astype(jnp.bfloat16)
    final_norm = norm_rows(final_rows, modulation[6], modulation[7]).astype(jnp.bfloat16)
    velocity = jnp.dot(final_norm, w_velocity, preferred_element_type=jnp.float32)
    noisy_own = lax.dynamic_slice_in_dim(noisy_mel, sub_index * own_rows, own_rows, 0)
    mel_own = noisy_own + 0.5 * velocity
    mel_next = lax.all_gather(mel_own, "sub", axis=0, tiled=True)
    mel_low = mel_next.astype(jnp.bfloat16)
    mel_wide = extended_2(mel_low, (("tm", 0),), 4)
    columns = frame_count + 2
    prelude = jnp.zeros((w_prelude.shape[1], columns), jnp.float32)
    for offset in range(7):
        prelude = prelude + lax.dot_general(
            w_prelude[offset],
            mel_wide[offset : offset + columns],
            (((1,), (1,)), ((), ())),
            preferred_element_type=jnp.float32,
        )
    frame_pos = time_index * frame_count - 1 + lax.broadcasted_iota(jnp.int32, (1, columns), 1)
    inside = (frame_pos >= 0) & (frame_pos < lax.axis_size("tm") * frame_count)
    prelude = jnp.where(inside, prelude, 0.0).astype(jnp.bfloat16)
    samples_dev = 4 * own_rows
    up_x = lax.psum_scatter(
        phase_terms(
            prelude, w_upsample, jnp.int32(0) // 4, samples_dev * lax.axis_size("sub") // 4
        ).astype(jnp.bfloat16),
        "sub",
        scatter_dimension=0,
        tiled=True,
    )
    act_one = snake_act(up_x.astype(jnp.float32), snake_alpha[0]).astype(jnp.bfloat16)
    wide_one = extended_2(act_one, ((("tm", "sub"), 0),), 3)
    inner_conv = dilated_conv(wide_one, samples_dev, w_dilated)
    act_two = snake_act(inner_conv, snake_alpha[1]).astype(jnp.bfloat16)
    wide_two = extended_2(act_two, ((("tm", "sub"), 0),), 1)
    outer_conv = plain_conv(wide_two, samples_dev, w_plain)
    section_out = (up_x.astype(jnp.float32) + outer_conv).astype(jnp.bfloat16)
    return (mel_next, section_out)


def solution(mesh):
    in_specs = (
        P(("tm", "sub"), None),
        P(),
        P(None, None, "sub"),
        P("sub", None),
        P(None, "sub"),
        P("sub", None),
        P(),
        P("tm", None),
        P(None, "sub", None),
        P(None, "sub", None),
        P(),
        P(None, "sub", None),
        P(None, "sub", None),
    )
    out_specs = (P("tm", None), P(("tm", "sub"), None))
    return jax.shard_map(body, mesh=mesh, in_specs=in_specs, out_specs=out_specs, check_vma=False)
```

profile of v0, /device:TPU:1, one launch (start us, length us, event | category | flops | bytes accessed | tf_op | source)
XLA Modules:
  0.0 477.0 jit_solution(3565787769455806827)
XLA Ops:
  8.1 1.1 slice_add_fusion
  9.2 41.1 %all-gather.5.cloned.1.call-done = bf16[1024,1024]{1,0:T(8,128)(2,1)} async-done(((bf16[64,1024]{1,0:T(8,128)(2,1)}), bf16[1024,1024]{1,0:T(8,128)(2,1)}) %all-gather.5.cloned.1.call-update) | async-done | bytes 2097168 | tf_op jit(solution)/shard_map/all_gather | solution.py:145
  50.2 2.4 convert_reduce_fusion
  52.7 2.2 fusion.14
  55.0 3.2 collective-permute-start.1
  58.6 3.2 collective-permute-start
  61.8 2.2 fusion.181
  64.0 2.1 fusion.29
  66.3 2.1 convolution_convert_fusion.1
  68.5 64.6 %reduce-scatter.4.cloned.1.call-done = bf16[64,1024]{1,0:T(8,128)(2,1)} async-done(((bf16[1024,1024]{1,0:T(8,128)(2,1)}), bf16[64,1024]{1,0:T(8,128)(2,1)}) %reduce-scatter.4.cloned.1.call-update) | async-done | bytes 131088 | tf_op jit(solution)/shard_map/reduce_scatter | solution.py:155
  133.1 1.1 convert_reduce_fusion.1
  134.2 0.8 fusion.84
  135.0 38.8 %all-gather.7.cloned.1.call-done = bf16[1024,1024]{1,0:T(8,128)(2,1)} async-done(((bf16[64,1024]{1,0:T(8,128)(2,1)}), bf16[1024,1024]{1,0:T(8,128)(2,1)}) %all-gather.7.cloned.1.call-update) | async-done | bytes 2097168 | tf_op jit(solution)/shard_map/all_gather | solution.py:163
  173.8 5.2 %convolution_convert_fusion = bf16[1024,1024]{1,0:T(8,128)(2,1)} fusion(bf16[256,1024]{1,0:T(8,128)(2,1)S(1)} %copy-done, bf16[1024,1024]{1,0:T(8,128)(2,1)} %all-gather.7.cloned.1.call-done, bf16[1024,256]{1,0:T(8,128)(2,1)S(1)} %copy-done.11), kind=kOutput, calls=%fused_computation.27 | convolution fusion | flops 1077149696 | bytes 5242880 | tf_op jit(solution)/shard_map/dot_general | solution.py:168
  179.1 1.0 constant_dynamic-slice_fusion
  180.1 62.5 %reduce-scatter.6.cloned.1.call-done = bf16[64,1024]{1,0:T(8,128)(2,1)} async-done(((bf16[1024,1024]{1,0:T(8,128)(2,1)}), bf16[64,1024]{1,0:T(8,128)(2,1)}) %reduce-scatter.6.cloned.1.call-update) | async-done | bytes 131088 | tf_op jit(solution)/shard_map/reduce_scatter | solution.py:167
  242.6 1.1 convert_reduce_fusion.2
  244.0 21.4 %all_gather.17 = f32[1024,100]{1,0:T(8,128)S(1)} all-gather(f32[64,100]{1,0:T(8,128)S(1)} %fusion.30), channel_id=1, replica_groups=mesh['tm'=16,'sub'=16] {'sub'}, dimensions={0}, use_global_device_ids=true | all-gather | bytes 435200 | tf_op jit(solution)/shard_map/all_gather | solution.py:178
  265.4 0.8 copy-done.2
  266.2 3.2 collective-permute-start.2
  269.5 1.5 collective-permute-start.3
  271.0 2.8 collective-permute-done.3
  273.8 0.7 concatenate.44
  276.3 0.7 copy-done.6
  277.0 0.7 fusion.114
  277.7 0.7 fusion.111
  278.4 0.7 fusion.108
  279.2 0.7 fusion.105
  281.1 0.7 fusion.19
  281.9 0.7 fusion.20
  282.6 0.8 pad_maximum_fusion
  283.4 7.5 %copy.33 = bf16[1024,4,768]{2,1,0:T(4,128)(2,1)} copy(bf16[1024,4,768]{2,0,1:T(8,128)(2,1)S(1)} %pad_maximum_fusion) | data formatting | bytes 12582912 | tf_op jit(solution)/shard_map/stack | solution.py:61
  290.9 10.7 %convert_element_type.111 = bf16[4096,768]{1,0:T(8,128)(2,1)} reshape(bf16[1024,4,768]{2,1,0:T(4,128)(2,1)} %copy.33) | data formatting | bytes 12582912 | tf_op jit(solution)/shard_map/convert_element_type | solution.py:197
  303.1 1.0 copy.34
  304.0 78.0 %reduce-scatter.8.cloned.1.call-done = bf16[256,768]{1,0:T(8,128)(2,1)} async-done(((bf16[4096,768]{1,0:T(8,128)(2,1)}), bf16[256,768]{1,0:T(8,128)(2,1)}) %reduce-scatter.8.cloned.1.call-update) | async-done | bytes 393232 | tf_op jit(solution)/shard_map/reduce_scatter | solution.py:194
  382.1 3.6 fusion.45
  385.7 1.9 collective-permute-start.5
  387.7 3.6 collective-permute-start.4
  391.3 32.0 %all-gather.9.cloned.1.call-done = bf16[3,768,768]{2,1,0:T(8,128)(2,1)} async-done(((bf16[3,48,768]{2,1,0:T(8,128)(2,1)}), bf16[3,768,768]{2,1,0:T(8,128)(2,1)}) %all-gather.9.cloned.1.call-update) | async-done | bytes 3538960 | tf_op jit(solution)/shard_map/all_gather | solution.py:104
  423.3 1.7 fusion.28
  425.0 1.8 fusion.27
  426.8 4.2 add_convert_fusion.4
  431.1 2.2 collective-permute-start.7
  433.3 3.5 collective-permute-start.6
  436.8 27.2 %all-gather.11.cloned.1.call-done = bf16[3,768,768]{2,1,0:T(8,128)(2,1)} async-done(((bf16[3,48,768]{2,1,0:T(8,128)(2,1)}), bf16[3,768,768]{2,1,0:T(8,128)(2,1)}) %all-gather.11.cloned.1.call-update) | async-done | bytes 3538960 | tf_op jit(solution)/shard_map/all_gather | solution.py:117
  464.0 1.7 fusion.26
  465.8 1.8 fusion.25
  467.6 2.5 fusion.24
  (83 shorter events, 6.4 us)
Async XLA Ops:
  7.2 166.6 %copy-start = (bf16[256,1024]{1,0:T(8,128)(2,1)S(1)}, bf16[256,1024]{1,0:T(8,128)(2,1)}, u32[]{:S(2)}) copy-start(bf16[256,1024]{1,0:T(8,128)(2,1)} %param.18) | copy-start | bytes 1572868
  7.2 43.1 %all-gather.5.cloned.1.call-start = ((), (), s32[]{:S(2)}) async-start(), calls=%async_computation.3 | async-start | bytes 2228224 | tf_op jit(solution)/shard_map/all_gather | solution.py:145
  7.9 125.2 %reduce-scatter.4.cloned.1.call-start = ((), (), s32[]{:S(2)}) async-start(), calls=%async_computation.4 | async-start | bytes 2228224 | tf_op jit(solution)/shard_map/reduce_scatter | solution.py:155
  50.2 2.4 copy-start.4
  55.0 6.8 %collective-permute-start.1 = (bf16[256,64]{0,1:T(8,128)(2,1)S(1)}, bf16[256,64]{0,1:T(8,128)(2,1)S(1)}, u32[]{:S(2)}, u32[]{:S(2)}) collective-permute-start(bf16[256,64]{0,1:T(8,128)(2,1)S(1)} %get-tuple-element.21), channel_id=1, source_target_pairs={{0,16},{16,32},{32,48},{48,64},{64,80},{80,96},{96,112},{112,128},... | collective-permute-start | bytes 98312 | tf_op jit(solution)/shard_map/ppermute | solution.py:15
  58.6 5.4 %collective-permute-start = (bf16[256,64]{0,1:T(8,128)(2,1)S(1)}, bf16[256,64]{0,1:T(8,128)(2,1)S(1)}, u32[]{:S(2)}, u32[]{:S(2)}) collective-permute-start(bf16[256,64]{0,1:T(8,128)(2,1)S(1)} %get-tuple-element.20), channel_id=1, source_target_pairs={{0,16},{16,32},{32,48},{48,64},{64,80},{80,96},{96,112},{112,128},... | collective-permute-start | bytes 98312 | tf_op jit(solution)/shard_map/ppermute | solution.py:15
  64.0 2.3 copy-start.9
  66.3 66.8 %copy-start.7 = (bf16[64,1024]{1,0:T(8,128)(2,1)S(1)}, bf16[64,1024]{1,0:T(8,128)(2,1)}, u32[]{:S(2)}) copy-start(bf16[64,1024]{1,0:T(8,128)(2,1)} %param.13) | copy-start | bytes 393220
  66.3 107.5 %copy-start.11 = (bf16[1024,256]{1,0:T(8,128)(2,1)S(1)}, bf16[1024,256]{1,0:T(8,128)(2,1)}, u32[]{:S(2)}) copy-start(bf16[1024,256]{1,0:T(8,128)(2,1)} %param.17) | copy-start | bytes 1572868
  68.4 105.4 %all-gather.7.cloned.1.call-start = ((), (), s32[]{:S(2)}) async-start(), calls=%async_computation.5 | async-start | bytes 2228224 | tf_op jit(solution)/shard_map/all_gather | solution.py:163
  135.0 107.7 %reduce-scatter.6.cloned.1.call-start = ((), (), s32[]{:S(2)}) async-start(), calls=%async_computation.6 | async-start | bytes 2228224 | tf_op jit(solution)/shard_map/reduce_scatter | solution.py:167
  179.0 64.7 %copy-start.12 = (bf16[1024,100]{0,1:T(8,128)(2,1)S(1)}, bf16[1024,100]{0,1:T(8,128)(2,1)}, u32[]{:S(2)}) copy-start(bf16[1024,100]{0,1:T(8,128)(2,1)} %param.19) | copy-start | bytes 614404
  179.0 95.5 %copy-start.8 = (bf16[7,96,100]{2,1,0:T(8,128)(2,1)S(1)}, bf16[7,96,100]{2,1,0:T(8,128)(2,1)}, u32[]{:S(2)}) copy-start(bf16[7,96,100]{2,1,0:T(8,128)(2,1)} %param.21) | copy-start | bytes 403204
  179.0 203.1 %reduce-scatter.8.cloned.1.call-start = ((), (), s32[]{:S(2)}) async-start(), calls=%async_computation.7 | async-start | bytes 6684672 | tf_op jit(solution)/shard_map/reduce_scatter | solution.py:194
  265.4 0.8 copy-start.2
  266.2 4.7 collective-permute-start.2
  269.5 4.3 collective-permute-start.3
  275.7 1.3 copy-start.6
  301.7 1.4 copy-start.10
  301.7 1.4 copy-start.3
  301.7 121.6 %all-gather.9.cloned.1.call-start = ((), (), s32[]{:S(2)}) async-start(), calls=%async_computation.8 | async-start | bytes 3760128 | tf_op jit(solution)/shard_map/all_gather | solution.py:104
  302.3 161.7 %all-gather.11.cloned.1.call-start = ((), (), s32[]{:S(2)}) async-start(), calls=%async_computation.9 | async-start | bytes 3760128 | tf_op jit(solution)/shard_map/all_gather | solution.py:117
  385.7 39.3 %collective-permute-start.5 = (bf16[3,768]{1,0:T(4,128)(2,1)S(1)}, bf16[3,768]{1,0:T(4,128)(2,1)S(1)}, u32[]{:S(2)}, u32[]{:S(2)}) collective-permute-start(bf16[3,768]{1,0:T(4,128)(2,1)S(1)} %get-tuple-element.19), channel_id=1, source_target_pairs={{1,0},{2,1},{3,2},{4,3},{5,4},{6,5},{7,6},{8,7},{9,8},{10,9},{11,1... | collective-permute-start | bytes 13832 | tf_op jit(solution)/shard_map/ppermute | solution.py:28
  387.7 39.1 %collective-permute-start.4 = (bf16[3,768]{1,0:T(4,128)(2,1)S(1)}, bf16[3,768]{1,0:T(4,128)(2,1)S(1)}, u32[]{:S(2)}, u32[]{:S(2)}) collective-permute-start(bf16[3,768]{1,0:T(4,128)(2,1)S(1)} %get-tuple-element.18), channel_id=1, source_target_pairs={{0,1},{1,2},{2,3},{3,4},{4,5},{5,6},{6,7},{7,8},{8,9},{9,10},{10,1... | collective-permute-start | bytes 13832 | tf_op jit(solution)/shard_map/ppermute | solution.py:26
  431.1 34.7 %collective-permute-start.7 = (bf16[1,768]{1,0:T(2,128)(2,1)S(1)}, bf16[1,768]{1,0:T(2,128)(2,1)S(1)}, u32[]{:S(2)}, u32[]{:S(2)}) collective-permute-start(bf16[1,768]{1,0:T(2,128)(2,1)S(1)} %get-tuple-element.17), channel_id=1, source_target_pairs={{1,0},{2,1},{3,2},{4,3},{5,4},{6,5},{7,6},{8,7},{9,8},{10,9},{11,1... | collective-permute-start | bytes 4616 | tf_op jit(solution)/shard_map/ppermute | solution.py:28
  433.3 34.3 %copy-start.5 = (bf16[256,768]{1,0:T(8,128)(2,1)S(1)}, bf16[256,768]{1,0:T(8,128)(2,1)}, u32[]{:S(2)}) copy-start(bf16[256,768]{1,0:T(8,128)(2,1)} %reduce-scatter.8.cloned.1.call-done) | copy-start | bytes 1179652
  433.3 34.3 %collective-permute-start.6 = (bf16[1,768]{1,0:T(2,128)(2,1)S(1)}, bf16[1,768]{1,0:T(2,128)(2,1)S(1)}, u32[]{:S(2)}, u32[]{:S(2)}) collective-permute-start(bf16[1,768]{1,0:T(2,128)(2,1)S(1)} %get-tuple-element.16), channel_id=1, source_target_pairs={{0,1},{1,2},{2,3},{3,4},{4,5},{5,6},{6,7},{7,8},{8,9},{9,10},{10,1... | collective-permute-start | bytes 4616 | tf_op jit(solution)/shard_map/ppermute | solution.py:26
  465.8 4.4 copy-start.1
Sparse Core Ops, SparseCore 0:
  9.8 40.3 all-gather.4
  68.5 64.4 reduce-scatter.3
  135.5 38.2 all-gather.6
  179.1 63.4 reduce-scatter.5
  301.8 80.2 reduce-scatter.7
  383.7 39.4 all-gather.8
  425.1 38.8 all-gather.10
where the time goes:
time: 478 us; the launch traced here: 477 us
  waiting for transfers between devices  349 us (73%)
  matrix products  35.1 us (7%)
  local copies, waits for them, and re-layouts  23.1 us (5%)
  starting transfers between devices  22.8 us (5%)
  blocking collectives  21.4 us (4%)
  between operations  14.7 us (3%)
  other arithmetic  11.1 us (2%)
    reduce_scatter x1, waiting for transfers between devices, body(): lax.psum_scatter(phase_terms(prelude, w_upsample, jnp.int32(0) // 4, samp...  78 us
    reduce_scatter x1, waiting for transfers between devices, body(): lax.psum_scatter(jnp.dot(heads_out, w_heads_out, preferred_element_type=j...  64.6 us
    reduce_scatter x1, waiting for transfers between devices, body(): lax.psum_scatter(jnp.dot(hidden, w_down, preferred_element_type=jnp.float...  62.5 us
    all_gather x1, waiting for transfers between devices, body(): gathered = lax.all_gather(frames, 'sub', axis=0, tiled=True)  41.1 us
    all_gather x1, waiting for transfers between devices, body(): second_norm = lax.all_gather(own_norm, 'sub', axis=0, tiled=True)  38.8 us
    all_gather x1, waiting for transfers between devices, dilated_conv(): weight_rows = lax.all_gather(w_dilated, 'sub', axis=1, tiled=True)  32 us
    all_gather x1, waiting for transfers between devices, plain_conv(): weight_rows = lax.all_gather(w_plain, 'sub', axis=1, tiled=True)  27.2 us
    all_gather x1, blocking collectives, body(): mel_next = lax.all_gather(mel_own, 'sub', axis=0, tiled=True)  21.4 us
  transfers between devices with their start and end apart: 15, of which 8 were waited for; matrix products, arithmetic and copies ran while one was open for 4% of the time, Pallas kernels for 0%

commit v1 on v0

--- a/solution.py
+++ b/solution.py
@@ -114,7 +114,10 @@
 def plain_conv(extended, row_count, w_plain):
     empty_sum = jnp.zeros((row_count, w_plain.shape[2]), jnp.float32)
     running = empty_sum
-    weight_rows = lax.all_gather(w_plain, "sub", axis=1, tiled=True)
+    size = lax.axis_size("sub")
+    shards = jnp.stack([w_plain for _ in range(size)])
+    shards = lax.all_to_all(shards, "sub", split_axis=0, concat_axis=0)
+    weight_rows = jnp.concatenate(shards, axis=1)
     for offset in range(3):
         running = running + jnp.dot(
             extended[offset : offset + row_count],

time: 478 us -> 497 us (1.040); the launches traced: 477 us -> 489 us
  starting transfers between devices: 22.8 us -> 27.8 us
    all_to_all x0 -> x1, waiting for transfers between devices: none -> 51.5 us  [plain_conv(): shards = lax.all_to_all(shards, 'sub', split_axis=0, concat_axis=0)]
    all_gather x1 -> x0, waiting for transfers between devices: 27.2 us -> none  [plain_conv(): weight_rows = lax.all_gather(w_plain, 'sub', axis=1, tiled=True)]
    reduce_scatter x1, waiting for transfers between devices: 78 us -> 54 us  [body(): lax.psum_scatter(phase_terms(prelude, w_upsample, jnp.int32(0) // 4, samp...]
    all_to_all x0 -> x1, starting transfers between devices: none -> 5.26 us  [plain_conv(): shards = lax.all_to_all(shards, 'sub', split_axis=0, concat_axis=0)]
  transfers between devices with their start and end apart: 15 -> 15, of which waited for: 8 -> 9; matrix products, arithmetic and copies ran while one was open for 4% -> 4% of each run, Pallas kernels for 0% -> 0%
where the time goes in v1:
time: 497 us; the launch traced here: 489 us
  waiting for transfers between devices  353 us (71%)
  matrix products  31.3 us (6%)
  starting transfers between devices  27.8 us (6%)
  local copies, waits for them, and re-layouts  27.7 us (6%)
  blocking collectives  22.9 us (5%)
  between operations  14.7 us (3%)
  other arithmetic  12.1 us (2%)
    reduce_scatter x1, waiting for transfers between devices, body(): lax.psum_scatter(jnp.dot(heads_out, w_heads_out, preferred_element_type=j...  64.6 us
    reduce_scatter x1, waiting for transfers between devices, body(): lax.psum_scatter(jnp.dot(hidden, w_down, preferred_element_type=jnp.float...  62.5 us
    reduce_scatter x1, waiting for transfers between devices, body(): lax.psum_scatter(phase_terms(prelude, w_upsample, jnp.int32(0) // 4, samp...  54 us
    all_to_all x1, waiting for transfers between devices, plain_conv(): shards = lax.all_to_all(shards, 'sub', split_axis=0, concat_axis=0)  51.5 us
    all_gather x1, waiting for transfers between devices, body(): gathered = lax.all_gather(frames, 'sub', axis=0, tiled=True)  41.1 us
    all_gather x1, waiting for transfers between devices, body(): second_norm = lax.all_gather(own_norm, 'sub', axis=0, tiled=True)  38.8 us
    all_gather x1, waiting for transfers between devices, dilated_conv(): weight_rows = lax.all_gather(w_dilated, 'sub', axis=1, tiled=True)  35.8 us
    all_gather x1, blocking collectives, body(): mel_next = lax.all_gather(mel_own, 'sub', axis=0, tiled=True)  22.9 us
  transfers between devices with their start and end apart: 15, of which 9 were waited for; matrix products, arithmetic and copies ran while one was open for 4% of the time, Pallas kernels for 0%

profile of v1, /device:TPU:1, one launch (start us, length us, event | category | flops | bytes accessed | tf_op | source)
XLA Modules:
  0.0 489.0 jit_solution(1018895861501357432)
XLA Ops:
  8.1 1.1 slice_add_fusion
  9.2 41.1 %all-gather.4.cloned.1.call-done = bf16[1024,1024]{1,0:T(8,128)(2,1)} async-done(((bf16[64,1024]{1,0:T(8,128)(2,1)}), bf16[1024,1024]{1,0:T(8,128)(2,1)}) %all-gather.4.cloned.1.call-update) | async-done | bytes 2097168 | tf_op jit(solution)/shard_map/all_gather | solution.py:148
  50.2 2.4 convert_reduce_fusion
  52.7 2.2 fusion.14
  55.0 3.2 collective-permute-start.1
  58.6 3.2 collective-permute-start
  61.8 2.2 fusion.181
  64.0 2.1 fusion.27
  66.3 2.1 convolution_convert_fusion.1
  68.5 64.6 %reduce-scatter.4.cloned.1.call-done = bf16[64,1024]{1,0:T(8,128)(2,1)} async-done(((bf16[1024,1024]{1,0:T(8,128)(2,1)}), bf16[64,1024]{1,0:T(8,128)(2,1)}) %reduce-scatter.4.cloned.1.call-update) | async-done | bytes 131088 | tf_op jit(solution)/shard_map/reduce_scatter | solution.py:158
  133.1 1.1 convert_reduce_fusion.1
  134.2 0.8 fusion.83
  135.0 38.8 %all-gather.6.cloned.1.call-done = bf16[1024,1024]{1,0:T(8,128)(2,1)} async-done(((bf16[64,1024]{1,0:T(8,128)(2,1)}), bf16[1024,1024]{1,0:T(8,128)(2,1)}) %all-gather.6.cloned.1.call-update) | async-done | bytes 2097168 | tf_op jit(solution)/shard_map/all_gather | solution.py:166
  173.8 5.2 %convolution_convert_fusion = bf16[1024,1024]{1,0:T(8,128)(2,1)} fusion(bf16[256,1024]{1,0:T(8,128)(2,1)S(1)} %copy-done, bf16[1024,1024]{1,0:T(8,128)(2,1)} %all-gather.6.cloned.1.call-done, bf16[1024,256]{1,0:T(8,128)(2,1)S(1)} %copy-done.13), kind=kOutput, calls=%fused_computation.27 | convolution fusion | flops 1077149696 | bytes 5242880 | tf_op jit(solution)/shard_map/dot_general | solution.py:171
  179.1 1.0 constant_dynamic-slice_fusion
  180.2 62.5 %reduce-scatter.6.cloned.1.call-done = bf16[64,1024]{1,0:T(8,128)(2,1)} async-done(((bf16[1024,1024]{1,0:T(8,128)(2,1)}), bf16[64,1024]{1,0:T(8,128)(2,1)}) %reduce-scatter.6.cloned.1.call-update) | async-done | bytes 131088 | tf_op jit(solution)/shard_map/reduce_scatter | solution.py:170
  242.6 1.1 convert_reduce_fusion.2
  244.0 22.9 %all_gather.14 = f32[1024,100]{1,0:T(8,128)} all-gather(f32[64,100]{1,0:T(8,128)S(1)} %fusion.28), channel_id=1, replica_groups=mesh['tm'=16,'sub'=16] {'sub'}, dimensions={0}, use_global_device_ids=true | all-gather | bytes 435200 | tf_op jit(solution)/shard_map/all_gather | solution.py:181
  266.9 1.1 convert_element_type.109
  268.0 3.2 collective-permute-start.2
  271.1 1.5 collective-permute-start.3
  272.6 2.8 collective-permute-done.3
  275.5 0.7 concatenate.44
  278.0 0.7 copy-done.7
  279.4 0.7 fusion.110
  280.1 0.7 fusion.107
  280.9 0.7 fusion.104
  282.8 0.7 fusion.19
  283.5 0.7 fusion.20
  284.3 0.8 pad_maximum_fusion
  285.1 7.5 %copy.33 = bf16[1024,4,768]{2,1,0:T(4,128)(2,1)} copy(bf16[1024,4,768]{2,0,1:T(8,128)(2,1)S(1)} %pad_maximum_fusion) | data formatting | bytes 12582912 | tf_op jit(solution)/shard_map/stack | solution.py:61
  292.6 10.7 %convert_element_type.111 = bf16[4096,768]{1,0:T(8,128)(2,1)} reshape(bf16[1024,4,768]{2,1,0:T(4,128)(2,1)} %copy.33) | data formatting | bytes 12582912 | tf_op jit(solution)/shard_map/convert_element_type | solution.py:200
  304.3 2.1 stack.44
  306.4 5.3 %all-to-all-start = ((bf16[16,3,48,768]{3,2,1,0:T(8,128)(2,1)}), bf16[16,3,48,768]{3,2,1,0:T(8,128)(2,1)S(1)}, u32[]{:S(2)}, u32[]{:S(2)}) async-start(bf16[16,3,48,768]{3,2,1,0:T(8,128)(2,1)} %stack.44), calls=%async_computation.3 | async-start | bytes 7077888 | tf_op jit(solution)/shard_map/all_to_all | solution.py:119
  311.6 51.5 %all-to-all-done = bf16[16,3,48,768]{3,2,1,0:T(8,128)(2,1)S(1)} async-done(((bf16[16,3,48,768]{3,2,1,0:T(8,128)(2,1)}), bf16[16,3,48,768]{3,2,1,0:T(8,128)(2,1)S(1)}, u32[]{:S(2)}, u32[]{:S(2)}) %all-to-all-start) | async-done | bytes 3538976 | tf_op jit(solution)/shard_map/all_to_all | solution.py:119
  363.2 1.9 fusion.175
  365.0 2.0 copy.34
  367.1 54.0 %reduce-scatter.8.cloned.1.call-done = bf16[256,768]{1,0:T(8,128)(2,1)} async-done(((bf16[4096,768]{1,0:T(8,128)(2,1)}), bf16[256,768]{1,0:T(8,128)(2,1)}) %reduce-scatter.8.cloned.1.call-update) | async-done | bytes 393232 | tf_op jit(solution)/shard_map/reduce_scatter | solution.py:197
  421.0 3.6 fusion.43
  424.7 3.2 collective-permute-start.5
  427.9 2.4 collective-permute-start.4
  430.3 35.8 %all-gather.8.cloned.1.call-done = bf16[3,768,768]{2,1,0:T(8,128)(2,1)} async-done(((bf16[3,48,768]{2,1,0:T(8,128)(2,1)}), bf16[3,768,768]{2,1,0:T(8,128)(2,1)}) %all-gather.8.cloned.1.call-update) | async-done | bytes 3538960 | tf_op jit(solution)/shard_map/all_gather | solution.py:104
  466.1 1.7 fusion.26
  467.8 1.8 fusion.25
  469.6 4.3 add_convert_fusion.4
  474.0 2.3 collective-permute-start.7
  476.8 3.4 collective-permute-start.6
  480.9 1.2 fusion.24
  (88 shorter events, 7.9 us)
Async XLA Ops:
  7.2 166.7 %copy-start = (bf16[256,1024]{1,0:T(8,128)(2,1)S(1)}, bf16[256,1024]{1,0:T(8,128)(2,1)}, u32[]{:S(2)}) copy-start(bf16[256,1024]{1,0:T(8,128)(2,1)} %param.18) | copy-start | bytes 1572868
  7.2 43.1 %all-gather.4.cloned.1.call-start = ((), (), s32[]{:S(2)}) async-start(), calls=%async_computation.4 | async-start | bytes 2228224 | tf_op jit(solution)/shard_map/all_gather | solution.py:148
  7.9 125.2 %reduce-scatter.4.cloned.1.call-start = ((), (), s32[]{:S(2)}) async-start(), calls=%async_computation.5 | async-start | bytes 2228224 | tf_op jit(solution)/shard_map/reduce_scatter | solution.py:158
  50.2 2.4 copy-start.5
  55.0 6.8 %collective-permute-start.1 = (bf16[256,64]{0,1:T(8,128)(2,1)S(1)}, bf16[256,64]{0,1:T(8,128)(2,1)S(1)}, u32[]{:S(2)}, u32[]{:S(2)}) collective-permute-start(bf16[256,64]{0,1:T(8,128)(2,1)S(1)} %get-tuple-element.24), channel_id=1, source_target_pairs={{0,16},{16,32},{32,48},{48,64},{64,80},{80,96},{96,112},{112,128},... | collective-permute-start | bytes 98312 | tf_op jit(solution)/shard_map/ppermute | solution.py:15
  58.6 5.4 %collective-permute-start = (bf16[256,64]{0,1:T(8,128)(2,1)S(1)}, bf16[256,64]{0,1:T(8,128)(2,1)S(1)}, u32[]{:S(2)}, u32[]{:S(2)}) collective-permute-start(bf16[256,64]{0,1:T(8,128)(2,1)S(1)} %get-tuple-element.23), channel_id=1, source_target_pairs={{0,16},{16,32},{32,48},{48,64},{64,80},{80,96},{96,112},{112,128},... | collective-permute-start | bytes 98312 | tf_op jit(solution)/shard_map/ppermute | solution.py:15
  64.0 2.3 copy-start.11
  66.3 66.8 %copy-start.8 = (bf16[64,1024]{1,0:T(8,128)(2,1)S(1)}, bf16[64,1024]{1,0:T(8,128)(2,1)}, u32[]{:S(2)}) copy-start(bf16[64,1024]{1,0:T(8,128)(2,1)} %param.13) | copy-start | bytes 393220
  66.3 107.5 %copy-start.13 = (bf16[1024,256]{1,0:T(8,128)(2,1)S(1)}, bf16[1024,256]{1,0:T(8,128)(2,1)}, u32[]{:S(2)}) copy-start(bf16[1024,256]{1,0:T(8,128)(2,1)} %param.17) | copy-start | bytes 1572868
  68.4 105.4 %all-gather.6.cloned.1.call-start = ((), (), s32[]{:S(2)}) async-start(), calls=%async_computation.6 | async-start | bytes 2228224 | tf_op jit(solution)/shard_map/all_gather | solution.py:166
  135.0 107.7 %reduce-scatter.6.cloned.1.call-start = ((), (), s32[]{:S(2)}) async-start(), calls=%async_computation.7 | async-start | bytes 2228224 | tf_op jit(solution)/shard_map/reduce_scatter | solution.py:170
  179.0 64.7 %copy-start.14 = (bf16[1024,100]{0,1:T(8,128)(2,1)S(1)}, bf16[1024,100]{0,1:T(8,128)(2,1)}, u32[]{:S(2)}) copy-start(bf16[1024,100]{0,1:T(8,128)(2,1)} %param.19) | copy-start | bytes 614404
  179.0 97.2 %copy-start.10 = (bf16[7,96,100]{2,1,0:T(8,128)(2,1)S(1)}, bf16[7,96,100]{2,1,0:T(8,128)(2,1)}, u32[]{:S(2)}) copy-start(bf16[7,96,100]{2,1,0:T(8,128)(2,1)} %param.21) | copy-start | bytes 403204
  179.0 242.0 %reduce-scatter.8.cloned.1.call-start = ((), (), s32[]{:S(2)}) async-start(), calls=%async_computation.8 | async-start | bytes 6684672 | tf_op jit(solution)/shard_map/reduce_scatter | solution.py:197
  268.0 4.7 collective-permute-start.2
  271.1 4.3 collective-permute-start.3
  277.4 1.3 copy-start.7
  303.3 0.9 copy-start.9
  303.3 162.7 %all-gather.8.cloned.1.call-start = ((), (), s32[]{:S(2)}) async-start(), calls=%async_computation.9 | async-start | bytes 3760128 | tf_op jit(solution)/shard_map/all_gather | solution.py:104
  306.4 5.3 %copy-start.12 = (f32[2,768]{1,0:T(2,128)S(1)}, f32[2,768]{1,0:T(2,128)}, u32[]{:S(2)}) copy-start(f32[2,768]{1,0:T(2,128)} %param.23) | copy-start | bytes 18436
  306.4 56.8 %all-to-all-start = ((bf16[16,3,48,768]{3,2,1,0:T(8,128)(2,1)}), bf16[16,3,48,768]{3,2,1,0:T(8,128)(2,1)S(1)}, u32[]{:S(2)}, u32[]{:S(2)}) async-start(bf16[16,3,48,768]{3,2,1,0:T(8,128)(2,1)} %stack.44), calls=%async_computation.3 | async-start | bytes 7077888 | tf_op jit(solution)/shard_map/all_to_all | solution.py:119
  424.7 43.1 %collective-permute-start.5 = (bf16[3,768]{1,0:T(4,128)(2,1)S(1)}, bf16[3,768]{1,0:T(4,128)(2,1)S(1)}, u32[]{:S(2)}, u32[]{:S(2)}) collective-permute-start(bf16[3,768]{1,0:T(4,128)(2,1)S(1)} %get-tuple-element.22), channel_id=1, source_target_pairs={{1,0},{2,1},{3,2},{4,3},{5,4},{6,5},{7,6},{8,7},{9,8},{10,9},{11,1... | collective-permute-start | bytes 13832 | tf_op jit(solution)/shard_map/ppermute | solution.py:28
  427.9 41.7 %collective-permute-start.4 = (bf16[3,768]{1,0:T(4,128)(2,1)S(1)}, bf16[3,768]{1,0:T(4,128)(2,1)S(1)}, u32[]{:S(2)}, u32[]{:S(2)}) collective-permute-start(bf16[3,768]{1,0:T(4,128)(2,1)S(1)} %get-tuple-element.21), channel_id=1, source_target_pairs={{0,1},{1,2},{2,3},{3,4},{4,5},{5,6},{6,7},{7,8},{8,9},{9,10},{10,1... | collective-permute-start | bytes 13832 | tf_op jit(solution)/shard_map/ppermute | solution.py:26
  469.6 6.7 %copy-start.3 = (bf16[1,16,48,768]{3,2,0,1:T(8,128)(2,1)S(1)}, bf16[1,16,48,768]{3,2,0,1:T(8,128)(2,1)}, u32[]{:S(2)}) copy-start(bf16[1,16,48,768]{3,2,0,1:T(8,128)(2,1)} %get-tuple-element.18) | copy-start | bytes 3538948
  474.0 6.3 %copy-start.2 = (bf16[1,16,48,768]{3,2,0,1:T(8,128)(2,1)S(1)}, bf16[1,16,48,768]{3,2,0,1:T(8,128)(2,1)}, u32[]{:S(2)}) copy-start(bf16[1,16,48,768]{3,2,0,1:T(8,128)(2,1)} %get-tuple-element.17) | copy-start | bytes 3538948
  474.0 6.2 %collective-permute-start.7 = (bf16[1,768]{1,0:T(2,128)(2,1)S(1)}, bf16[1,768]{1,0:T(2,128)(2,1)S(1)}, u32[]{:S(2)}, u32[]{:S(2)}) collective-permute-start(bf16[1,768]{1,0:T(2,128)(2,1)S(1)} %get-tuple-element.20), channel_id=1, source_target_pairs={{1,0},{2,1},{3,2},{4,3},{5,4},{6,5},{7,6},{8,7},{9,8},{10,9},{11,1... | collective-permute-start | bytes 4616 | tf_op jit(solution)/shard_map/ppermute | solution.py:28
  476.3 4.6 copy-start.4
  476.4 4.6 copy-start.6
  476.8 4.1 collective-permute-start.6
  480.2 1.9 copy-start.1
Sparse Core Ops, SparseCore 0:
  9.8 40.3 all-gather.3
  68.5 64.4 reduce-scatter.3
  135.5 38.2 all-gather.5
  179.2 63.4 reduce-scatter.5
  303.5 117.5 reduce-scatter.7
  422.7 43.3 all-gather.7
